TPU v7x, 256 devices: a whole 4x4x8 slice. The times are simulated.
256 devices in a mesh: grp: 16 (over z, core), ing: 16 (over y, x).
Axes of the slice: x: 4, y: 4, z: 8, core: 2. Of those that a mesh axis runs over, the one named last changes fastest.
Arguments:
- amplitudes: bfloat16 [512, 800, 800], P('grp', 'ing'), may hold values from -6 to 6
- integrals: bfloat16 [512, 800, 800], P('grp', 'ing'), may hold values from -0.0024414062 to 0.0024414062
- fock_block: bfloat16 [800, 800], P('ing'), may hold values from -0.625 to 0.625
- virtual_irrep: int32 [800], replicated, may hold values from 0 to 7, as said below
- pair_irrep: int32 [512], P(('grp', 'ing')), may hold values from 0 to 7
- pair_energy: float32 [512], P(('grp', 'ing')), may hold values from -4 to -1
- virtual_energy: float32 [800], replicated, may hold values from 0.5 to 4
Outputs:
- update: float32 [512, 800, 800], P('grp', 'ing')
Inputs may be any that keep to these rules, and one draw needn't show every extreme that they name: `virtual_irrep`: the orbitals of one irreducible representation form one contiguous run of 100 plus or minus at most 25 orbitals, and all 8 representations occur.
All inputs are finite; a program needn't handle non-finite values.
Results may differ from a plain program's by a relative error of at most 0.0029.
Values may be sent and summed in bfloat16 or wider, within the bound.
A program may use at most 128 MiB of HBM per device.

v0:
```python
import jax
import jax.numpy as jnp
from jax import lax
from jax.sharding import PartitionSpec as P


def symmetry_mask(values, pair_irrep, virtual_irrep):
    allowed = (
        jnp.bitwise_xor(virtual_irrep[:, None], virtual_irrep[None, :])[None]
        == pair_irrep[:, None, None]
    )
    return jnp.where(allowed, values, jnp.zeros_like(values))


def body(amplitudes, integrals, fock_block, virtual_irrep, pair_irrep, pair_energy, virtual_energy):
    same_irrep = virtual_irrep[:, None] == virtual_irrep[None, :]
    whole_amps, whole_ints = (
        lax.all_to_all(amplitudes, "ing", split_axis=0, concat_axis=1, tiled=True),
        lax.all_to_all(integrals, "ing", split_axis=0, concat_axis=1, tiled=True),
    )
    amp_masked = symmetry_mask(whole_amps, pair_irrep, virtual_irrep)
    int_masked = symmetry_mask(whole_ints, pair_irrep, virtual_irrep)
    partial_value = jnp.einsum(
        "paf,pef->ae", amp_masked, int_masked, preferred_element_type=jnp.float32
    )
    correction = lax.psum(partial_value, ("grp", "ing"))
    fock_full = lax.all_gather(fock_block, "ing", axis=0, tiled=True)
    fock_part = jnp.where(
        same_irrep, fock_full.astype(jnp.float32), jnp.zeros(fock_full.shape, jnp.float32)
    )
    operator_vv = (fock_part + correction).astype(jnp.bfloat16)
    product = jnp.einsum("pae,be->pab", amp_masked, operator_vv, preferred_element_type=jnp.float32)
    denominator = (
        pair_energy[:, None, None] - virtual_energy[None, :, None] - virtual_energy[None, None, :]
    )
    scaled = (product - jnp.swapaxes(product, 1, 2)) / denominator
    return lax.all_to_all(scaled, "ing", split_axis=1, concat_axis=0, tiled=True)


def solution(mesh):
    in_specs = (
        P("grp", "ing", None),
        P("grp", "ing", None),
        P("ing", None),
        P(),
        P(("grp", "ing")),
        P(("grp", "ing")),
        P(),
    )
    out_specs = P("grp", "ing", None)
    return jax.shard_map(body, mesh=mesh, in_specs=in_specs, out_specs=out_specs, check_vma=False)
```

profile of v0, /device:TPU:99, one launch (start us, length us, event | category | flops | bytes accessed | tf_op | source)
XLA Modules:
  0.0 516.4 jit_solution(2653213600742417975)
XLA Ops:
  7.4 4.4 copy.25
  11.8 6.9 %all-to-all-start = ((bf16[32,50,800]{2,1,0:T(8,128)(2,1)}), bf16[32,50,800]{2,1,0:T(8,128)(2,1)S(1)}, u32[]{:S(2)}, u32[]{:S(2)}) async-start(bf16[32,50,800]{2,1,0:T(8,128)(2,1)} %copy.25), calls=%async_computation | async-start | bytes 6422528 | tf_op jit(solution)/shard_map/all_to_all | solution.py:18
  18.7 4.5 copy.27
  23.2 0.0 copy-start.2
  23.2 39.1 %all-to-all-done = bf16[32,50,800]{2,1,0:T(8,128)(2,1)S(1)} async-done(((bf16[32,50,800]{2,1,0:T(8,128)(2,1)}), bf16[32,50,800]{2,1,0:T(8,128)(2,1)S(1)}, u32[]{:S(2)}, u32[]{:S(2)}) %all-to-all-start) | async-done | bytes 2560032 | tf_op jit(solution)/shard_map/all_to_all | solution.py:18
  62.3 8.3 %all-to-all-start.1 = ((bf16[32,50,800]{2,1,0:T(8,128)(2,1)}), bf16[32,50,800]{2,1,0:T(8,128)(2,1)}, u32[]{:S(2)}, u32[]{:S(2)}) async-start(bf16[32,50,800]{2,1,0:T(8,128)(2,1)} %copy.27), calls=%async_computation.1 | async-start | bytes 6422528 | tf_op jit(solution)/shard_map/all_to_all | solution.py:19
  70.7 0.0 all-gather.3.cloned.1.call-start
  70.7 0.7 all-gather.3.cloned.1.call-update
  71.4 0.0 all-reduce.2.cloned.1.call-start
  71.4 0.0 copy-done.2
  71.5 1.8 broadcast_xor_fusion
  73.3 3.8 copy.26
  77.1 35.5 %all-to-all-done.1 = bf16[32,50,800]{2,1,0:T(8,128)(2,1)} async-done(((bf16[32,50,800]{2,1,0:T(8,128)(2,1)}), bf16[32,50,800]{2,1,0:T(8,128)(2,1)}, u32[]{:S(2)}, u32[]{:S(2)}) %all-to-all-start.1) | async-done | bytes 2560032 | tf_op jit(solution)/shard_map/all_to_all | solution.py:19
  112.6 0.0 copy-start
  112.6 0.0 copy-start.1
  112.6 0.0 copy-start.4
  112.6 4.3 copy.28
  116.9 0.0 copy-done
  116.9 0.0 copy-done.1
  116.9 0.0 copy-done.4
  116.9 7.2 %compare_select_fusion = (bf16[2,800,800]{2,0,1:T(2,128)(2,1)S(1)}, bf16[2,800,800]{2,0,1:T(2,128)(2,1)S(1)}) fusion(bf16[16,2,50,800]{3,1,2,0:T(2,128)(2,1)S(1)} %copy.28, s32[800,800]{1,0:T(8,128)S(1)} %copy-done, s32[2]{0:T(128)S(1)} %copy-done.4, bf16[16,2,50,800]{3,1,2,0:T(2,128)(2,1)S(1)} %copy-done.1), kind=kLoop, calls=%fused_computation | loop fusion | flops 3840000 | bytes 12800008 | tf_op jit(solution)/shard_map/jit(_where)/select_n | solution.py:12
  124.1 4.8 fusion.6
  129.0 0.0 copy-start.3
  129.0 0.0 copy-start.5
  129.0 0.0 all-reduce.2.cloned.1.call-update
  129.0 0.7 copy-done.3
  129.7 0.0 copy-done.5
  129.7 0.1 broadcast_subtract_fusion
  129.7 9.6 %all-gather.3.cloned.1.call-done = bf16[16,50,800]{2,1,0:T(8,128)(2,1)} async-done(((bf16[1,50,800]{2,1,0:T(8,128)(2,1)}), bf16[16,50,800]{2,1,0:T(8,128)(2,1)}) %all-gather.3.cloned.1.call-update) | async-done | bytes 1280016 | tf_op jit(solution)/shard_map/all_gather | solution.py:27
  139.3 3.0 reshape.63
  142.4 254.5 %all-reduce.2.cloned.1.call-done = f32[800,800]{1,0:T(8,128)} async-done(((f32[800,800]{1,0:T(8,128)}), f32[800,800]{1,0:T(8,128)}) %all-reduce.2.cloned.1.call-update) | async-done | bytes 2560016 | tf_op jit(solution)/shard_map/psum | solution.py:26
  396.8 8.1 %fusion.4 = f32[2,800,800]{2,1,0:T(8,128)} fusion(bf16[2,800,800]{2,0,1:T(2,128)(2,1)S(1)} %get-tuple-element.6, f32[800,800]{1,0:T(8,128)} %all-reduce.2.cloned.1.call-done, f32[800,800]{1,0:T(8,128)} %reshape.63, s32[800]{0:T(1024)S(1)} %copy-done.2), kind=kOutput, calls=%fused_computation.8 | convolution fusion | flops 2050560000 | bytes 12803200 | tf_op jit(solution)/shard_map/pae,be->pab/dot_general | solution.py:32
  404.9 7.1 %copy.32 = f32[2,800,800]{1,2,0:T(8,128)} copy(f32[2,800,800]{2,1,0:T(8,128)} %fusion.4) | data formatting | bytes 10240000 | tf_op jit(solution)/shard_map/pae,be->pab/dot_general | solution.py:32
  412.0 5.1 fusion
  417.1 4.4 copy.33
  421.5 73.9 %all_to_all.54 = f32[2,800,800]{2,0,1:T(2,128)S(1)} all-to-all(f32[2,800,800]{2,0,1:T(2,128)S(1)} %copy.33), channel_id=1, replica_groups=mesh['grp'=16,'ing'=16] {'ing'}, dimensions={1} | all-to-all | bytes 10240000 | tf_op jit(solution)/shard_map/all_to_all | solution.py:37
  495.4 5.7 %copy.34 = f32[16,2,50,800]{3,1,0,2:T(2,128)} copy(f32[16,2,50,800]{3,1,2,0:T(2,128)S(1)} %bitcast.25) | data formatting | bytes 10240000 | tf_op jit(solution)/shard_map/all_to_all | solution.py:37
  501.1 7.8 %all_to_all.50 = f32[32,50,800]{2,0,1:T(8,128)} reshape(f32[16,2,50,800]{3,1,0,2:T(2,128)} %copy.34) | data formatting | bytes 10240000 | tf_op jit(solution)/shard_map/all_to_all | solution.py:37
Async XLA Ops:
  11.8 50.5 %all-to-all-start = ((bf16[32,50,800]{2,1,0:T(8,128)(2,1)}), bf16[32,50,800]{2,1,0:T(8,128)(2,1)S(1)}, u32[]{:S(2)}, u32[]{:S(2)}) async-start(bf16[32,50,800]{2,1,0:T(8,128)(2,1)} %copy.25), calls=%async_computation | async-start | bytes 6422528 | tf_op jit(solution)/shard_map/all_to_all | solution.py:18
  23.2 48.2 %copy-start.2 = (s32[800]{0:T(1024)S(1)}, s32[800]{0:T(1024)}, u32[]{:S(2)}) copy-start(s32[800]{0:T(1024)} %param.10) | copy-start | bytes 9604
  62.3 50.3 %all-to-all-start.1 = ((bf16[32,50,800]{2,1,0:T(8,128)(2,1)}), bf16[32,50,800]{2,1,0:T(8,128)(2,1)}, u32[]{:S(2)}, u32[]{:S(2)}) async-start(bf16[32,50,800]{2,1,0:T(8,128)(2,1)} %copy.27), calls=%async_computation.1 | async-start | bytes 6422528 | tf_op jit(solution)/shard_map/all_to_all | solution.py:19
  70.7 68.7 %all-gather.3.cloned.1.call-start = ((), (), s32[]{:S(2)}) async-start(), calls=%async_computation.4 | async-start | bytes 1705984 | tf_op jit(solution)/shard_map/all_gather | solution.py:27
  71.4 325.4 %all-reduce.2.cloned.1.call-start = ((), (), s32[]{:S(2)}) async-start(), calls=%async_computation.3 | async-start | bytes 5734400 | tf_op jit(solution)/shard_map/psum | solution.py:26
  112.6 4.3 copy-start
  112.6 4.3 copy-start.1
  112.6 4.3 copy-start.4
  129.0 0.7 copy-start.3
  129.0 0.7 copy-start.5
Sparse Core Ops, SparseCore 0:
  74.2 65.0 all-gather.2
Sparse Core Ops, SparseCore 1:
  129.1 267.7 all-reduce.1
where the time goes:
time: 517 us; the launch traced here: 516 us
  waiting for transfers between devices  339 us (66%)
  blocking collectives  73.9 us (14%)
  local copies, waits for them, and re-layouts  45.7 us (9%)
  starting transfers between devices  15.3 us (3%)
  between operations  14.9 us (3%)
  other arithmetic  14.3 us (3%)
  matrix products  12.9 us (2%)
    psum x1, waiting for transfers between devices, body(): correction = lax.psum(partial_value, ('grp', 'ing'))  254 us
    all_to_all x1, blocking collectives, body(): lax.all_to_all(scaled, 'ing', split_axis=1, concat_axis=0, tiled=True)  73.9 us
    all_to_all x1, waiting for transfers between devices, body(): lax.all_to_all(amplitudes, 'ing', split_axis=0, concat_axis=1, tiled=True)  39.1 us
    all_to_all x1, waiting for transfers between devices, body(): lax.all_to_all(integrals, 'ing', split_axis=0, concat_axis=1, tiled=True)  35.5 us
    all_to_all x2, local copies, waits for them, and re-layouts, body(): lax.all_to_all(scaled, 'ing', split_axis=1, concat_axis=0, tiled=True)  13.5 us
  transfers between devices with their start and end apart: 4, of which 4 were waited for; matrix products, arithmetic and copies ran while one was open for 6% of the time, Pallas kernels for 0%

commit v1 on v0

--- a/solution.py
+++ b/solution.py
@@ -23,7 +23,7 @@
     partial_value = jnp.einsum(
         "paf,pef->ae", amp_masked, int_masked, preferred_element_type=jnp.float32
     )
-    correction = lax.psum(partial_value, ("grp", "ing"))
+    correction = lax.psum(lax.psum(partial_value, "grp"), "ing")
     fock_full = lax.all_gather(fock_block, "ing", axis=0, tiled=True)
     fock_part = jnp.where(
         same_irrep, fock_full.astype(jnp.float32), jnp.zeros(fock_full.shape, jnp.float32)

time: 517 us -> 474 us (0.917)
  waiting for transfers between devices: 339 us -> 295 us
    psum x1 -> x2, waiting for transfers between devices: 254 us -> 220 us  [body(): correction = lax.psum(lax.psum(partial_value, 'grp'), 'ing')]
    all_gather x1, waiting for transfers between devices: 9.61 us -> 0.01 us  [body(): fock_full = lax.all_gather(fock_block, 'ing', axis=0, tiled=True)]
  transfers between devices with their start and end apart: 4 -> 5, of which waited for: 4 -> 4; matrix products, arithmetic and copies ran while one was open for 6% -> 3% of each run, Pallas kernels for 0% -> 0%
where the time goes in v1:
time: 474 us; the launch traced here: 470 us
  waiting for transfers between devices  295 us (62%)
  blocking collectives  71.9 us (15%)
  local copies, waits for them, and re-layouts  45.1 us (10%)
  starting transfers between devices  15.8 us (3%)
  between operations  14.9 us (3%)
  other arithmetic  14.1 us (3%)
  matrix products  12.9 us (3%)
    psum x2, waiting for transfers between devices, body(): correction = lax.psum(lax.psum(partial_value, 'grp'), 'ing')  220 us
    all_to_all x1, blocking collectives, body(): lax.all_to_all(scaled, 'ing', split_axis=1, concat_axis=0, tiled=True)  71.9 us
    all_to_all x1, waiting for transfers between devices, body(): lax.all_to_all(amplitudes, 'ing', split_axis=0, concat_axis=1, tiled=True)  39.1 us
    all_to_all x1, waiting for transfers between devices, body(): lax.all_to_all(integrals, 'ing', split_axis=0, concat_axis=1, tiled=True)  35.2 us
    all_to_all x2, local copies, waits for them, and re-layouts, body(): lax.all_to_all(scaled, 'ing', split_axis=1, concat_axis=0, tiled=True)  13.5 us
  transfers between devices with their start and end apart: 5, of which 4 were waited for; matrix products, arithmetic and copies ran while one was open for 3% of the time, Pallas kernels for 0%

profile of v1, /device:TPU:99, one launch (start us, length us, event | category | flops | bytes accessed | tf_op | source)
XLA Modules:
  0.0 469.7 jit_solution(5832382185796731040)
XLA Ops:
  7.4 4.4 copy.25
  11.8 6.9 %all-to-all-start = ((bf16[32,50,800]{2,1,0:T(8,128)(2,1)}), bf16[32,50,800]{2,1,0:T(8,128)(2,1)S(1)}, u32[]{:S(2)}, u32[]{:S(2)}) async-start(bf16[32,50,800]{2,1,0:T(8,128)(2,1)} %copy.25), calls=%async_computation | async-start | bytes 6422528 | tf_op jit(solution)/shard_map/all_to_all | solution.py:18
  18.7 4.5 copy.27
  23.2 0.0 copy-start.2
  23.2 39.1 %all-to-all-done = bf16[32,50,800]{2,1,0:T(8,128)(2,1)S(1)} async-done(((bf16[32,50,800]{2,1,0:T(8,128)(2,1)}), bf16[32,50,800]{2,1,0:T(8,128)(2,1)S(1)}, u32[]{:S(2)}, u32[]{:S(2)}) %all-to-all-start) | async-done | bytes 2560032 | tf_op jit(solution)/shard_map/all_to_all | solution.py:18
  62.3 8.3 %all-to-all-start.1 = ((bf16[32,50,800]{2,1,0:T(8,128)(2,1)}), bf16[32,50,800]{2,1,0:T(8,128)(2,1)}, u32[]{:S(2)}, u32[]{:S(2)}) async-start(bf16[32,50,800]{2,1,0:T(8,128)(2,1)} %copy.27), calls=%async_computation.1 | async-start | bytes 6422528 | tf_op jit(solution)/shard_map/all_to_all | solution.py:19
  70.7 0.2 all-reduce.3.cloned.1.call-start
  70.9 0.0 copy-done.2
  70.9 1.8 broadcast_xor_fusion
  72.7 3.8 copy.26
  76.6 35.2 %all-to-all-done.1 = bf16[32,50,800]{2,1,0:T(8,128)(2,1)} async-done(((bf16[32,50,800]{2,1,0:T(8,128)(2,1)}), bf16[32,50,800]{2,1,0:T(8,128)(2,1)}, u32[]{:S(2)}, u32[]{:S(2)}) %all-to-all-start.1) | async-done | bytes 2560032 | tf_op jit(solution)/shard_map/all_to_all | solution.py:19
  111.8 0.0 copy-start
  111.8 0.0 copy-start.1
  111.8 0.0 copy-start.4
  111.8 4.3 copy.28
  116.1 0.0 copy-done
  116.1 0.0 copy-done.1
  116.1 0.0 copy-done.4
  116.1 7.0 %compare_select_fusion = (bf16[2,800,800]{2,0,1:T(2,128)(2,1)S(1)}, bf16[2,800,800]{2,0,1:T(2,128)(2,1)S(1)}) fusion(bf16[16,2,50,800]{3,1,2,0:T(2,128)(2,1)S(1)} %copy.28, s32[800,800]{1,0:T(8,128)S(1)} %copy-done, s32[2]{0:T(128)S(1)} %copy-done.4, bf16[16,2,50,800]{3,1,2,0:T(2,128)(2,1)S(1)} %copy-done.1), kind=kLoop, calls=%fused_computation | loop fusion | flops 3840000 | bytes 12800008 | tf_op jit(solution)/shard_map/jit(_where)/select_n | solution.py:12
  123.2 4.8 %fusion.6 = f32[800,800]{1,0:T(8,128)} fusion(bf16[2,800,800]{2,0,1:T(2,128)(2,1)S(1)} %get-tuple-element.5, bf16[2,800,800]{2,0,1:T(2,128)(2,1)S(1)} %get-tuple-element.6), kind=kOutput, calls=%fused_computation.10 | convolution fusion | flops 2048000000 | bytes 7680000 | tf_op jit(solution)/shard_map/paf,pef->ae/dot_general | solution.py:23
  128.0 0.0 copy-start.3
  128.0 0.0 copy-start.5
  128.0 0.0 all-reduce.3.cloned.1.call-update
  128.0 0.0 all-gather.3.cloned.1.call-start
  128.1 0.5 all-gather.3.cloned.1.call-update
  128.6 0.3 all-reduce.5.cloned.1.call-start
  128.9 121.1 %all-reduce.3.cloned.1.call-done = f32[800,800]{1,0:T(8,128)} async-done(((f32[800,800]{1,0:T(8,128)}), f32[800,800]{1,0:T(8,128)}) %all-reduce.3.cloned.1.call-update) | async-done | bytes 2560016 | tf_op jit(solution)/shard_map/psum | solution.py:26
  249.9 0.0 all-reduce.5.cloned.1.call-update
  249.9 0.0 copy-done.3
  249.9 0.0 copy-done.5
  250.0 0.1 broadcast_subtract_fusion
  250.0 0.0 all-gather.3.cloned.1.call-done
  250.0 3.0 reshape.63
  253.1 99.1 %all-reduce.5.cloned.1.call-done = f32[800,800]{1,0:T(8,128)} async-done(((f32[800,800]{1,0:T(8,128)}), f32[800,800]{1,0:T(8,128)}) %all-reduce.5.cloned.1.call-update) | async-done | bytes 2560016 | tf_op jit(solution)/shard_map/psum | solution.py:26
  352.1 8.1 %fusion.4 = f32[2,800,800]{2,1,0:T(8,128)} fusion(bf16[2,800,800]{2,0,1:T(2,128)(2,1)S(1)} %get-tuple-element.6, f32[800,800]{1,0:T(8,128)} %all-reduce.5.cloned.1.call-done, f32[800,800]{1,0:T(8,128)} %reshape.63, s32[800]{0:T(1024)S(1)} %copy-done.2), kind=kOutput, calls=%fused_computation.8 | convolution fusion | flops 2050560000 | bytes 12803200 | tf_op jit(solution)/shard_map/pae,be->pab/dot_general | solution.py:32
  360.2 7.1 %copy.32 = f32[2,800,800]{1,2,0:T(8,128)} copy(f32[2,800,800]{2,1,0:T(8,128)} %fusion.4) | data formatting | bytes 10240000 | tf_op jit(solution)/shard_map/pae,be->pab/dot_general | solution.py:32
  367.3 5.1 %fusion = f32[2,800,800]{2,1,0:T(8,128)S(1)} fusion(f32[2,800,800]{2,1,0:T(8,128)} %fusion.4, f32[2,800,800]{1,2,0:T(8,128)} %copy.32, f32[800]{0:T(1024)S(1)} %copy-done.3, f32[2,800]{1,0:T(2,128)S(1)} %broadcast_subtract_fusion), kind=kLoop, calls=%fused_computation.3 | loop fusion | flops 3840000 | bytes 15369600 | tf_op jit(solution)/shard_map/div | solution.py:36
  372.4 4.4 copy.33
  376.9 71.9 %all_to_all.54 = f32[2,800,800]{2,0,1:T(2,128)S(1)} all-to-all(f32[2,800,800]{2,0,1:T(2,128)S(1)} %copy.33), channel_id=1, replica_groups=mesh['grp'=16,'ing'=16] {'ing'}, dimensions={1} | all-to-all | bytes 10240000 | tf_op jit(solution)/shard_map/all_to_all | solution.py:37
  448.7 5.7 %copy.34 = f32[16,2,50,800]{3,1,0,2:T(2,128)} copy(f32[16,2,50,800]{3,1,2,0:T(2,128)S(1)} %bitcast.25) | data formatting | bytes 10240000 | tf_op jit(solution)/shard_map/all_to_all | solution.py:37
  454.4 7.8 %all_to_all.50 = f32[32,50,800]{2,0,1:T(8,128)} reshape(f32[16,2,50,800]{3,1,0,2:T(2,128)} %copy.34) | data formatting | bytes 10240000 | tf_op jit(solution)/shard_map/all_to_all | solution.py:37
Async XLA Ops:
  11.8 50.5 %all-to-all-start = ((bf16[32,50,800]{2,1,0:T(8,128)(2,1)}), bf16[32,50,800]{2,1,0:T(8,128)(2,1)S(1)}, u32[]{:S(2)}, u32[]{:S(2)}) async-start(bf16[32,50,800]{2,1,0:T(8,128)(2,1)} %copy.25), calls=%async_computation | async-start | bytes 6422528 | tf_op jit(solution)/shard_map/all_to_all | solution.py:18
  23.2 47.7 %copy-start.2 = (s32[800]{0:T(1024)S(1)}, s32[800]{0:T(1024)}, u32[]{:S(2)}) copy-start(s32[800]{0:T(1024)} %param.10) | copy-start | bytes 9604
  62.3 49.5 %all-to-all-start.1 = ((bf16[32,50,800]{2,1,0:T(8,128)(2,1)}), bf16[32,50,800]{2,1,0:T(8,128)(2,1)}, u32[]{:S(2)}, u32[]{:S(2)}) async-start(bf16[32,50,800]{2,1,0:T(8,128)(2,1)} %copy.27), calls=%async_computation.1 | async-start | bytes 6422528 | tf_op jit(solution)/shard_map/all_to_all | solution.py:19
  70.7 179.3 %all-reduce.3.cloned.1.call-start = ((), (), s32[]{:S(2)}) async-start(), calls=%async_computation.3 | async-start | bytes 5734400 | tf_op jit(solution)/shard_map/psum | solution.py:26
  111.8 4.3 copy-start
  111.8 4.3 copy-start.1
  111.8 4.3 copy-start.4
  128.0 122.0 %copy-start.3 = (f32[800]{0:T(1024)S(1)}, f32[800]{0:T(1024)}, u32[]{:S(2)}) copy-start(f32[800]{0:T(1024)} %param.13) | copy-start | bytes 9604
  128.0 122.0 %copy-start.5 = (f32[2]{0:T(128)S(1)}, f32[2]{0:T(128)}, u32[]{:S(2)}) copy-start(f32[2]{0:T(128)} %param.12) | copy-start | bytes 28
  128.0 122.0 %all-gather.3.cloned.1.call-start = ((), (), s32[]{:S(2)}) async-start(), calls=%async_computation.5 | async-start | bytes 1705984 | tf_op jit(solution)/shard_map/all_gather | solution.py:27
  128.6 223.6 %all-reduce.5.cloned.1.call-start = ((), (), s32[]{:S(2)}) async-start(), calls=%async_computation.4 | async-start | bytes 5734400 | tf_op jit(solution)/shard_map/psum | solution.py:26
Sparse Core Ops, SparseCore 0:
  128.1 121.7 all-reduce.2
Sparse Core Ops, SparseCore 1:
  130.9 51.1 all-gather.2
  250.0 102.1 all-reduce.4
